TPU v7x, 512 devices: a whole 4x4x16 slice. The times are simulated.
512 devices in a mesh: clusters: 32 (over z, core), group: 16 (over x, y).
Axes of the slice: x: 4, y: 4, z: 16, core: 2. Of those that a mesh axis runs over, the one named last changes fastest.
Arguments:
- embeddings: bfloat16 [262144, 1024], P(('clusters', 'group')), may hold values from -20 to 20
- new_label: int32 [262144], P(('clusters', 'group')), may hold values from 0 to 31, as said below
- dest_member: int32 [262144], P(('clusters', 'group')), may hold values from 0 to 15, as said below
- seed_index: int32 [32, 512], P('clusters'), may hold values from 0 to 8191, as said below
- kappa: float32 [32], P('clusters'), may hold values from 8 to 400
Outputs:
- centroids: bfloat16 [16384, 1024], P('clusters')
- row_score: float32 [524288], P(('clusters', 'group'))
Inputs may be any that keep to these rules, and one draw needn't show every extreme that they name: `new_label`: each device sends between 192 and 320 of its rows to devices of other coarse clusters, at most 1 to any one device; in every draw one device receives exactly 1 row from every device of the other clusters, and every device sends exactly 1 row to some device. Rows whose label is their own device's cluster stay. `dest_member`: A row whose new_label is its own device's cluster has its own device's index along group here. `seed_index`: the 512 entries of cluster c are distinct positions m * 512 + s among the rows held before the move by cluster c's devices (m along group, s the row on that device), each naming a row whose new_label is c.
All inputs are finite; a program needn't handle non-finite values.
Results may differ from a plain program's by a relative error of at most 0.02.
The roundings to bfloat16 on the way count: a program that leaves them out, or rounds other values in their place, can miss the bound.
Values may be sent and summed in bfloat16 or wider, within the bound.
A program may use at most 64 MiB of HBM per device.

v0:
```python
import jax
import jax.numpy as jnp
from jax import lax
from jax.sharding import PartitionSpec as P

ITERS = 2
EPSILON = 1e-06


def unit_rows(embedded):
    values = embedded.astype(jnp.float32)
    scale = lax.rsqrt(jnp.sum(values * values, axis=-1, keepdims=True) + EPSILON)
    return (values * scale).astype(jnp.bfloat16)


def expectation(normed, alive, centres, concentration):
    scores = concentration * jnp.einsum(
        "sd,kd->sk", normed, centres, preferred_element_type=jnp.float32
    )
    largest = jnp.max(scores, axis=-1, keepdims=True)
    powered = jnp.exp(scores - largest)
    summed = jnp.sum(powered, axis=-1, keepdims=True)
    weights = (powered / summed * alive[:, None]).astype(jnp.bfloat16)
    log_norm = (largest[:, 0] + jnp.log(summed[:, 0])) * alive
    return (weights, log_norm)


def normalise(summed):
    length = jnp.sqrt(jnp.sum(summed * summed, axis=-1, keepdims=True))
    return (summed / jnp.maximum(length, 1.0)).astype(jnp.bfloat16)


def outgoing_rows(normed, moving, target, capacity, device_count):
    row_count = normed.shape[0]
    positions = jnp.arange(row_count, dtype=jnp.int32)
    matches = (
        (target[:, None] == target[None, :])
        & (positions[None, :] < positions[:, None])
        & moving[None, :]
    )
    earlier = jnp.sum(matches, axis=1)
    slot_index = jnp.where(moving, target * capacity + earlier, device_count * capacity)
    source_row = (
        jnp.full((device_count * capacity,), row_count, jnp.int32)
        .at[slot_index]
        .set(positions, mode="drop")
    )
    padded = jnp.concatenate([normed, jnp.zeros((1, normed.shape[1]), jnp.bfloat16)], axis=0)
    return (padded[source_row], (source_row < row_count).astype(jnp.bfloat16))


def shards(embeddings, new_label, dest_member, seed_index, kappa):
    row_count, feature_width = embeddings.shape
    cluster_count = lax.axis_size("clusters")
    member_count = lax.axis_size("group")
    device_count = cluster_count * member_count
    own_cluster = lax.axis_index("clusters")
    own_member = lax.axis_index("group")
    movers_most = row_count * 5 // 8
    other_devices = (cluster_count - 1) * member_count
    capacity = (movers_most + other_devices - 1) // other_devices
    normed = unit_rows(embeddings)
    moving = new_label != own_cluster
    target = new_label * member_count + dest_member
    leaving, filled = outgoing_rows(normed, moving, target, capacity, device_count)
    leaving = leaving.reshape(cluster_count, member_count, capacity, feature_width)
    filled = filled.reshape(cluster_count, member_count, capacity)
    arrived, occupied = (
        lax.all_to_all(
            lax.all_to_all(leaving, "clusters", split_axis=0, concat_axis=0, tiled=True),
            "group",
            split_axis=1,
            concat_axis=1,
            tiled=True,
        ),
        lax.all_to_all(
            lax.all_to_all(filled, "clusters", split_axis=0, concat_axis=0, tiled=True),
            "group",
            split_axis=1,
            concat_axis=1,
            tiled=True,
        ),
    )
    seed_rows = seed_index.reshape(-1)
    local_pos = seed_rows - own_member * row_count
    held_here = (local_pos >= 0) & (local_pos < row_count)
    chosen = jnp.where(
        held_here[:, None],
        normed[jnp.clip(local_pos, 0, row_count - 1)],
        jnp.zeros((), jnp.bfloat16),
    )
    centres = lax.psum(chosen.astype(jnp.float32).astype(jnp.bfloat16), "group")
    concentration = kappa[0]
    incoming = arrived.reshape(-1, feature_width)
    alive_in = occupied.reshape(-1).astype(jnp.float32)
    alive_own = jnp.where(moving, 0.0, 1.0).astype(jnp.float32)
    norm_own = alive_own
    norm_in = alive_in
    for iteration in range(ITERS):
        weights_own, norm_own = expectation(normed, alive_own, centres, concentration)
        weights_in, norm_in = expectation(incoming, alive_in, centres, concentration)
        partial_value = jnp.einsum(
            "sk,sd->kd", weights_own, normed, preferred_element_type=jnp.float32
        )
        partial_value = partial_value + jnp.einsum(
            "sk,sd->kd", weights_in, incoming, preferred_element_type=jnp.float32
        )
        centres = normalise(
            lax.psum(partial_value.astype(jnp.bfloat16), "group").astype(jnp.float32)
        )
    return (centres, jnp.concatenate([norm_own, norm_in]))


def solution(mesh):
    return jax.shard_map(
        shards,
        mesh=mesh,
        in_specs=(
            P(("clusters", "group"), None),
            P(("clusters", "group")),
            P(("clusters", "group")),
            P("clusters", None),
            P("clusters"),
        ),
        out_specs=(P("clusters", None), P(("clusters", "group"))),
        check_vma=False,
    )
```

profile of v0, /device:TPU:32, one launch (start us, length us, event | category | flops | bytes accessed | tf_op | source)
XLA Modules:
  0.0 431.6 jit_solution(14022457909516345308)
XLA Ops:
  8.8 2.4 scatter_custom_fusion
  12.0 15.4 %all-to-all-start.2 = ((bf16[32,16,1]{1,2,0:T(2,128)(2,1)}), bf16[32,16,1]{1,2,0:T(2,128)(2,1)S(1)}, u32[]{:S(2)}, u32[]{:S(2)}) async-start(bf16[32,16,1]{1,2,0:T(2,128)(2,1)} %reshape.128), calls=%async_computation.2 | async-start | bytes 32768 | tf_op jit(solution)/shard_map/all_to_all | solution.py:77
  27.4 1.5 fusion
  28.9 1.5 fusion.1
  30.5 2.8 gather_fusion.1
  33.2 5.3 %all-to-all-done.2 = bf16[32,16,1]{1,2,0:T(2,128)(2,1)S(1)} async-done(((bf16[32,16,1]{1,2,0:T(2,128)(2,1)}), bf16[32,16,1]{1,2,0:T(2,128)(2,1)S(1)}, u32[]{:S(2)}, u32[]{:S(2)}) %all-to-all-start.2) | async-done | bytes 1056 | tf_op jit(solution)/shard_map/all_to_all | solution.py:77
  38.6 7.0 %all-to-all-start = ((bf16[32,16,1,1024]{3,1,2,0:T(8,128)(2,1)}), bf16[32,16,1,1024]{3,1,2,0:T(8,128)(2,1)S(1)}, u32[]{:S(2)}, u32[]{:S(2)}) async-start(bf16[32,16,1,1024]{3,1,2,0:T(8,128)(2,1)} %bitcast.4), calls=%async_computation | async-start | bytes 2097152 | tf_op jit(solution)/shard_map/all_to_all | solution.py:70
  45.7 2.1 gather_fusion
  49.6 50.1 %all-to-all-done = bf16[32,16,1,1024]{3,1,2,0:T(8,128)(2,1)S(1)} async-done(((bf16[32,16,1,1024]{3,1,2,0:T(8,128)(2,1)}), bf16[32,16,1,1024]{3,1,2,0:T(8,128)(2,1)S(1)}, u32[]{:S(2)}, u32[]{:S(2)}) %all-to-all-start) | async-done | bytes 1048608 | tf_op jit(solution)/shard_map/all_to_all | solution.py:70
  99.7 7.0 %all-to-all-start.3 = ((bf16[32,16,1]{0,2,1:T(2,128)(2,1)}), bf16[32,16,1]{0,2,1:T(2,128)(2,1)S(1)}, u32[]{:S(2)}, u32[]{:S(2)}) async-start(bf16[32,16,1]{0,2,1:T(2,128)(2,1)} %copy.28), calls=%async_computation.3 | async-start | bytes 16384 | tf_op jit(solution)/shard_map/all_to_all | solution.py:76
  107.4 1.6 copy.25
  109.0 5.4 %all-to-all-done.3 = bf16[32,16,1]{0,2,1:T(2,128)(2,1)S(1)} async-done(((bf16[32,16,1]{0,2,1:T(2,128)(2,1)}), bf16[32,16,1]{0,2,1:T(2,128)(2,1)S(1)}, u32[]{:S(2)}, u32[]{:S(2)}) %all-to-all-start.3) | async-done | bytes 1056 | tf_op jit(solution)/shard_map/all_to_all | solution.py:76
  114.3 3.7 all-to-all-start.1
  118.2 51.1 %all-reduce.5.cloned.1.call-done = bf16[512,1024]{1,0:T(8,128)(2,1)} async-done(((bf16[512,1024]{1,0:T(8,128)(2,1)}), bf16[512,1024]{1,0:T(8,128)(2,1)}) %all-reduce.5.cloned.1.call-update) | async-done | bytes 1048592 | tf_op jit(solution)/shard_map/psum | solution.py:92
  169.3 2.0 fusion.30
  171.5 2.1 fusion.12
  176.4 1.7 add_convert_fusion.1
  178.4 117.4 %all-reduce.7.cloned.1.call-done = bf16[512,1024]{1,0:T(8,128)(2,1)} async-done(((bf16[512,1024]{1,0:T(8,128)(2,1)}), bf16[512,1024]{1,0:T(8,128)(2,1)}) %all-reduce.7.cloned.1.call-update) | async-done | bytes 1048592 | tf_op jit(solution)/shard_map/psum | solution.py:109
  295.7 1.5 fusion.2
  297.2 2.0 fusion.32
  301.7 1.7 add_convert_fusion
  304.0 117.0 %all-reduce.9.cloned.1.call-done = bf16[512,1024]{1,0:T(8,128)(2,1)} async-done(((bf16[512,1024]{1,0:T(8,128)(2,1)}), bf16[512,1024]{1,0:T(8,128)(2,1)}) %all-reduce.9.cloned.1.call-update) | async-done | bytes 1048592 | tf_op jit(solution)/shard_map/psum | solution.py:109
  421.0 1.5 fusion.4
  422.5 2.5 fusion.5
  (46 shorter events, 10.8 us)
Async XLA Ops:
  12.0 26.6 %all-to-all-start.2 = ((bf16[32,16,1]{1,2,0:T(2,128)(2,1)}), bf16[32,16,1]{1,2,0:T(2,128)(2,1)S(1)}, u32[]{:S(2)}, u32[]{:S(2)}) async-start(bf16[32,16,1]{1,2,0:T(2,128)(2,1)} %reshape.128), calls=%async_computation.2 | async-start | bytes 32768 | tf_op jit(solution)/shard_map/all_to_all | solution.py:77
  33.2 12.4 %copy-start.1 = (s32[1,512]{1,0:T(1,128)S(1)}, s32[1,512]{1,0:T(1,128)}, u32[]{:S(2)}) copy-start(s32[1,512]{1,0:T(1,128)} %param.8) | copy-start | bytes 6148
  38.6 61.1 %all-to-all-start = ((bf16[32,16,1,1024]{3,1,2,0:T(8,128)(2,1)}), bf16[32,16,1,1024]{3,1,2,0:T(8,128)(2,1)S(1)}, u32[]{:S(2)}, u32[]{:S(2)}) async-start(bf16[32,16,1,1024]{3,1,2,0:T(8,128)(2,1)} %bitcast.4), calls=%async_computation | async-start | bytes 2097152 | tf_op jit(solution)/shard_map/all_to_all | solution.py:70
  45.6 123.8 %all-reduce.5.cloned.1.call-start = ((), (), s32[]{:S(2)}) async-start(), calls=%async_computation.4 | async-start | bytes 2097152 | tf_op jit(solution)/shard_map/psum | solution.py:92
  99.7 14.6 %all-to-all-start.3 = ((bf16[32,16,1]{0,2,1:T(2,128)(2,1)}), bf16[32,16,1]{0,2,1:T(2,128)(2,1)S(1)}, u32[]{:S(2)}, u32[]{:S(2)}) async-start(bf16[32,16,1]{0,2,1:T(2,128)(2,1)} %copy.28), calls=%async_computation.3 | async-start | bytes 16384 | tf_op jit(solution)/shard_map/all_to_all | solution.py:76
  114.3 59.2 %all-to-all-start.1 = ((bf16[32,16,1,1024]{3,0,2,1:T(8,128)(2,1)}), bf16[32,16,1,1024]{3,0,2,1:T(8,128)(2,1)S(1)}, u32[]{:S(2)}, u32[]{:S(2)}) async-start(bf16[32,16,1,1024]{3,0,2,1:T(8,128)(2,1)} %copy.25), calls=%async_computation.1 | async-start | bytes 2097152 | tf_op jit(solution)/shard_map/all_to_all | solution.py:69
  118.0 177.7 %all-reduce.7.cloned.1.call-start = ((), (), s32[]{:S(2)}) async-start(), calls=%async_computation.5 | async-start | bytes 2097152 | tf_op jit(solution)/shard_map/psum | solution.py:109
  173.6 1.2 copy-start.2
  174.8 1.6 copy-start.3
  178.1 242.9 %all-reduce.9.cloned.1.call-start = ((), (), s32[]{:S(2)}) async-start(), calls=%async_computation.6 | async-start | bytes 2097152 | tf_op jit(solution)/shard_map/psum | solution.py:109
  299.4 1.2 copy-start
Sparse Core Ops, SparseCore 0:
  50.2 119.0 all-reduce.4
  178.3 117.4 all-reduce.6
  303.5 117.4 all-reduce.8
where the time goes:
time: 432 us
  waiting for transfers between devices  346 us (80%)
  starting transfers between devices  33.4 us (8%)
  between operations  14.6 us (3%)
  other arithmetic  12.8 us (3%)
  local copies, waits for them, and re-layouts  12.8 us (3%)
  matrix products  11.7 us (3%)
    psum x2, waiting for transfers between devices, shards(): lax.psum(partial_value.astype(jnp.bfloat16), 'group').astype(jnp.float32)  234 us
    psum x1, waiting for transfers between devices, shards(): centres = lax.psum(chosen.astype(jnp.float32).astype(jnp.bfloat16), 'group')  51.1 us
    all_to_all x1, waiting for transfers between devices, shards(): lax.all_to_all(leaving, 'clusters', split_axis=0, concat_axis=0, tiled=True)  50.1 us
    all_to_all x1, starting transfers between devices, shards(): lax.all_to_all(filled, 'clusters', split_axis=0, concat_axis=0, tiled=True)  15.4 us
  transfers between devices with their start and end apart: 7, of which 6 were waited for; matrix products, arithmetic and copies ran while one was open for 4% of the time, Pallas kernels for 0%

commit v1 on v0

--- a/solution.py
+++ b/solution.py
@@ -66,12 +66,22 @@
     leaving = leaving.reshape(cluster_count, member_count, capacity, feature_width)
     filled = filled.reshape(cluster_count, member_count, capacity)
     arrived, occupied = (
-        lax.all_to_all(
-            lax.all_to_all(leaving, "clusters", split_axis=0, concat_axis=0, tiled=True),
-            "group",
-            split_axis=1,
-            concat_axis=1,
-            tiled=True,
+        jnp.concatenate(
+            lax.all_to_all(
+                jnp.stack(
+                    jnp.split(
+                        lax.all_to_all(
+                            leaving, "clusters", split_axis=0, concat_axis=0, tiled=True
+                        ),
+                        lax.axis_size("group"),
+                        axis=1,
+                    )
+                ),
+                "group",
+                0,
+                0,
+            ),
+            axis=1,
         ),
         lax.all_to_all(
             lax.all_to_all(filled, "clusters", split_axis=0, concat_axis=0, tiled=True),

time: 432 us -> 435 us (level)
  waiting for transfers between devices: 346 us -> 334 us
  local copies, waits for them, and re-layouts: 12.8 us -> 23.8 us
    unnamed x8 -> x23, local copies, waits for them, and re-layouts: 1.79 us -> 11.4 us
    psum x1, waiting for transfers between devices: 51.1 us -> 45 us  [shards(): centres = lax.psum(chosen.astype(jnp.float32).astype(jnp.bfloat16), 'group')]
    all_to_all x1, waiting for transfers between devices: 5.38 us -> 0.01 us  [shards(): lax.all_to_all(lax.all_to_all(filled, 'clusters', split_axis=0, concat_ax...]
  transfers between devices with their start and end apart: 7 -> 7, of which waited for: 6 -> 5; matrix products, arithmetic and copies ran while one was open for 4% -> 6% of each run, Pallas kernels for 0% -> 0%
where the time goes in v1:
time: 435 us; the launch traced here: 434 us
  waiting for transfers between devices  334 us (77%)
  starting transfers between devices  36.9 us (8%)
  local copies, waits for them, and re-layouts  23.8 us (5%)
  between operations  14.6 us (3%)
  other arithmetic  12.8 us (3%)
  matrix products  11.8 us (3%)
    psum x2, waiting for transfers between devices, shards(): lax.psum(partial_value.astype(jnp.bfloat16), 'group').astype(jnp.float32)  234 us
    all_to_all x1, waiting for transfers between devices, shards(): lax.all_to_all(leaving, 'clusters', split_axis=0, concat_axis=0, tiled=True)  49.5 us
    psum x1, waiting for transfers between devices, shards(): centres = lax.psum(chosen.astype(jnp.float32).astype(jnp.bfloat16), 'group')  45 us
    all_to_all x1, starting transfers between devices, shards(): lax.all_to_all(filled, 'clusters', split_axis=0, concat_axis=0, tiled=True)  15.4 us
    unnamed x23, local copies, waits for them, and re-layouts  11.4 us
  transfers between devices with their start and end apart: 7, of which 5 were waited for; matrix products, arithmetic and copies ran while one was open for 6% of the time, Pallas kernels for 0%

profile of v1, /device:TPU:32, one launch (start us, length us, event | category | flops | bytes accessed | tf_op | source)
XLA Modules:
  0.0 434.0 jit_solution(15847107451881946460)
XLA Ops:
  8.8 2.4 scatter_custom_fusion
  12.0 15.4 %all-to-all-start.2 = ((bf16[32,16,1]{1,2,0:T(2,128)(2,1)}), bf16[32,16,1]{1,2,0:T(2,128)(2,1)S(1)}, u32[]{:S(2)}, u32[]{:S(2)}) async-start(bf16[32,16,1]{1,2,0:T(2,128)(2,1)} %reshape.128), calls=%async_computation.2 | async-start | bytes 32768 | tf_op jit(solution)/shard_map/all_to_all | solution.py:87
  27.4 1.5 fusion
  28.9 1.5 fusion.1
  30.5 2.8 gather_fusion.1
  33.2 5.3 %all-to-all-done.2 = bf16[32,16,1]{1,2,0:T(2,128)(2,1)S(1)} async-done(((bf16[32,16,1]{1,2,0:T(2,128)(2,1)}), bf16[32,16,1]{1,2,0:T(2,128)(2,1)S(1)}, u32[]{:S(2)}, u32[]{:S(2)}) %all-to-all-start.2) | async-done | bytes 1056 | tf_op jit(solution)/shard_map/all_to_all | solution.py:87
  38.6 7.0 %all-to-all-start = ((bf16[32,16,1,1024]{3,1,2,0:T(8,128)(2,1)}), bf16[32,16,1,1024]{3,1,2,0:T(8,128)(2,1)S(1)}, u32[]{:S(2)}, u32[]{:S(2)}) async-start(bf16[32,16,1,1024]{3,1,2,0:T(8,128)(2,1)} %bitcast.4), calls=%async_computation | async-start | bytes 2097152 | tf_op jit(solution)/shard_map/all_to_all | solution.py:73
  45.7 2.1 gather_fusion
  47.8 1.1 broadcast_select_fusion
  50.2 49.5 %all-to-all-done = bf16[32,16,1,1024]{3,1,2,0:T(8,128)(2,1)S(1)} async-done(((bf16[32,16,1,1024]{3,1,2,0:T(8,128)(2,1)}), bf16[32,16,1,1024]{3,1,2,0:T(8,128)(2,1)S(1)}, u32[]{:S(2)}, u32[]{:S(2)}) %all-to-all-start) | async-done | bytes 1048608 | tf_op jit(solution)/shard_map/all_to_all | solution.py:73
  99.7 7.0 %all-to-all-start.3 = ((bf16[32,16,1]{0,2,1:T(2,128)(2,1)}), bf16[32,16,1]{0,2,1:T(2,128)(2,1)S(1)}, u32[]{:S(2)}, u32[]{:S(2)}) async-start(bf16[32,16,1]{0,2,1:T(2,128)(2,1)} %copy.106), calls=%async_computation.3 | async-start | bytes 16384 | tf_op jit(solution)/shard_map/all_to_all | solution.py:86
  106.7 2.3 fusion.46
  119.3 7.2 %all-to-all-start.1 = ((bf16[16,32,1,1,1024]{4,1,3,2,0:T(8,128)(2,1)}), bf16[16,32,1,1,1024]{4,1,3,2,0:T(8,128)(2,1)S(1)}, u32[]{:S(2)}, u32[]{:S(2)}) async-start(bf16[16,32,1,1,1024]{4,1,3,2,0:T(8,128)(2,1)} %fusion.26), calls=%async_computation.1 | async-start | bytes 2097152 | tf_op jit(solution)/shard_map/all_to_all | solution.py:70
  126.7 45.0 %all-reduce.5.cloned.1.call-done = bf16[512,1024]{1,0:T(8,128)(2,1)} async-done(((bf16[512,1024]{1,0:T(8,128)(2,1)}), bf16[512,1024]{1,0:T(8,128)(2,1)}) %all-reduce.5.cloned.1.call-update) | async-done | bytes 1048592 | tf_op jit(solution)/shard_map/psum | solution.py:102
  171.7 2.0 fusion.47
  173.9 2.1 fusion.12
  178.8 1.7 add_convert_fusion.1
  180.7 117.4 %all-reduce.7.cloned.1.call-done = bf16[512,1024]{1,0:T(8,128)(2,1)} async-done(((bf16[512,1024]{1,0:T(8,128)(2,1)}), bf16[512,1024]{1,0:T(8,128)(2,1)}) %all-reduce.7.cloned.1.call-update) | async-done | bytes 1048592 | tf_op jit(solution)/shard_map/psum | solution.py:119
  298.1 1.5 fusion.2
  299.6 2.0 fusion.49
  304.0 1.7 add_convert_fusion
  306.4 117.0 %all-reduce.9.cloned.1.call-done = bf16[512,1024]{1,0:T(8,128)(2,1)} async-done(((bf16[512,1024]{1,0:T(8,128)(2,1)}), bf16[512,1024]{1,0:T(8,128)(2,1)}) %all-reduce.9.cloned.1.call-update) | async-done | bytes 1048592 | tf_op jit(solution)/shard_map/psum | solution.py:119
  423.4 1.5 fusion.4
  424.9 2.5 fusion.5
  (62 shorter events, 20.0 us)
Async XLA Ops:
  12.0 26.6 %all-to-all-start.2 = ((bf16[32,16,1]{1,2,0:T(2,128)(2,1)}), bf16[32,16,1]{1,2,0:T(2,128)(2,1)S(1)}, u32[]{:S(2)}, u32[]{:S(2)}) async-start(bf16[32,16,1]{1,2,0:T(2,128)(2,1)} %reshape.128), calls=%async_computation.2 | async-start | bytes 32768 | tf_op jit(solution)/shard_map/all_to_all | solution.py:87
  33.2 12.4 %copy-start.1 = (s32[1,512]{1,0:T(1,128)S(1)}, s32[1,512]{1,0:T(1,128)}, u32[]{:S(2)}) copy-start(s32[1,512]{1,0:T(1,128)} %param.8) | copy-start | bytes 6148
  38.6 61.1 %all-to-all-start = ((bf16[32,16,1,1024]{3,1,2,0:T(8,128)(2,1)}), bf16[32,16,1,1024]{3,1,2,0:T(8,128)(2,1)S(1)}, u32[]{:S(2)}, u32[]{:S(2)}) async-start(bf16[32,16,1,1024]{3,1,2,0:T(8,128)(2,1)} %bitcast.4), calls=%async_computation | async-start | bytes 2097152 | tf_op jit(solution)/shard_map/all_to_all | solution.py:73
  45.6 126.1 %all-reduce.5.cloned.1.call-start = ((), (), s32[]{:S(2)}) async-start(), calls=%async_computation.4 | async-start | bytes 2097152 | tf_op jit(solution)/shard_map/psum | solution.py:102
  99.7 19.6 %all-to-all-start.3 = ((bf16[32,16,1]{0,2,1:T(2,128)(2,1)}), bf16[32,16,1]{0,2,1:T(2,128)(2,1)S(1)}, u32[]{:S(2)}, u32[]{:S(2)}) async-start(bf16[32,16,1]{0,2,1:T(2,128)(2,1)} %copy.106), calls=%async_computation.3 | async-start | bytes 16384 | tf_op jit(solution)/shard_map/all_to_all | solution.py:86
  119.3 56.7 %all-to-all-start.1 = ((bf16[16,32,1,1,1024]{4,1,3,2,0:T(8,128)(2,1)}), bf16[16,32,1,1,1024]{4,1,3,2,0:T(8,128)(2,1)S(1)}, u32[]{:S(2)}, u32[]{:S(2)}) async-start(bf16[16,32,1,1,1024]{4,1,3,2,0:T(8,128)(2,1)} %fusion.26), calls=%async_computation.1 | async-start | bytes 2097152 | tf_op jit(solution)/shard_map/all_to_all | solution.py:70
  126.5 171.6 %all-reduce.7.cloned.1.call-start = ((), (), s32[]{:S(2)}) async-start(), calls=%async_computation.5 | async-start | bytes 2097152 | tf_op jit(solution)/shard_map/psum | solution.py:119
  176.0 1.2 copy-start.2
  177.2 1.6 copy-start.3
  180.5 242.9 %all-reduce.9.cloned.1.call-start = ((), (), s32[]{:S(2)}) async-start(), calls=%async_computation.6 | async-start | bytes 2097152 | tf_op jit(solution)/shard_map/psum | solution.py:119
  301.8 1.2 copy-start
Sparse Core Ops, SparseCore 0:
  50.2 121.4 all-reduce.4
  180.6 117.4 all-reduce.6
  305.9 117.4 all-reduce.8
